TPU v7x, 512 devices: a whole 4x8x8 slice. The times are simulated.
512 devices in a mesh: seq: 128 (over y, z, core), mp: 4 (over x).
Axes of the slice: x: 4, y: 8, z: 8, core: 2. Of those that a mesh axis runs over, the one named last changes fastest.
Arguments:
- fresh_queries: bfloat16 [8192, 2048], P('seq', 'mp'), may hold values from -120 to 120
- fresh_keys: bfloat16 [8192, 1024], P('seq', 'mp'), may hold values from -6 to 6
- fresh_values: bfloat16 [8192, 1024], P('seq', 'mp'), may hold values from -6 to 6
- cache: bfloat16 [2, 8192, 1024], P(None, 'seq', 'mp'), may hold values from -6 to 6
- pool_root: int32 [128, 32], replicated, may hold values from 0 to 31
- branch_owner: int32 [128], replicated, may hold values from 0 to 127, each once
- branch_len: int32 [128], replicated, may hold values from 1 to 32, 2048 in all
- branch_root: int32 [128], replicated, may hold values from 0 to 31
- request_branch: int32 [128, 4], P('seq'), may hold values from 0 to 127
- token_request: int32 [128, 64], P('seq'), may hold values from 0 to 3, never falling along the last dimension, each value on 1 to 32 neighbouring positions
- residual: bfloat16 [8192, 2048], P('seq'), may hold values from -1.5 to 1.5
- wo_t: bfloat16 [2048, 2048], P('seq', 'mp'), may hold values from -0.125 to 0.125
- norm_gain: float32 [2048], replicated, may hold values from 0.1 to 1.9
- w_qkv: bfloat16 [2048, 4096], P('seq', 'mp'), may hold values from -0.125 to 0.125
Outputs:
- attn: bfloat16 [8192, 2048], P('seq', 'mp')
- stream: bfloat16 [8192, 2048], P('seq')
- qkv_next: bfloat16 [8192, 4096], P('seq', 'mp')
Inputs may be any that keep to these rules, and one draw needn't show every extreme that they name: `token_request`: in each index's row the request number never falls, and each request has 1 to 32 tokens. `branch_owner`: each index of seq holds exactly one branch. `branch_len`: the longest branch has 32 rows.
All inputs are finite; a program needn't handle non-finite values.
Results may differ from a plain program's by a relative error of at most 0.018.
Values may be sent and summed in bfloat16 or wider, within the bound.
A program may use at most 64 MiB of HBM per device.

v0:
```python
import jax
import jax.numpy as jnp
from jax import lax
from jax.sharding import PartitionSpec as P

QUERY_HEADS = 16
KEY_VALUE_HEADS = 8
HEAD_SIZE = 128


def cache_tags(pool_root, branch_owner, branch_len, root_count, slot_count):
    owner_count = pool_root.shape[0]
    branch_count = branch_owner.shape[0]
    branch_ids = jnp.arange(branch_count, dtype=jnp.int32)
    owner_ids = jnp.arange(owner_count, dtype=jnp.int32)
    owned = jnp.sum(
        jnp.where(branch_owner[None, :] == owner_ids[:, None], branch_ids[None, :], 0), axis=1
    )
    owned_length = jnp.sum(
        jnp.where(branch_ids[None, :] == owned[:, None], branch_len[None, :], 0), axis=1
    )
    slot_ids = jnp.arange(slot_count, dtype=jnp.int32)
    branch_tags = jnp.where(
        slot_ids[None, :] < owned_length[:, None], root_count + owned[:, None], -1
    )
    return jnp.concatenate([pool_root, branch_tags], axis=1).reshape(-1)


def absorb(running, query_rows, key_row_block, value_rows, visible, score_scale):
    peak_old, total, mixed = running
    scores = (
        jnp.einsum("tkgd,rkd->tkgr", query_rows, key_row_block, preferred_element_type=jnp.float32)
        * score_scale
    )
    seen = visible[:, None, None, :]
    peak_new = jnp.maximum(peak_old, jnp.max(jnp.where(seen, scores, -jnp.inf), axis=-1))
    factor = jnp.exp(peak_old - peak_new)
    weights_full = jnp.where(seen, jnp.exp(scores - peak_new[..., None]), 0.0)
    total = total * factor + jnp.sum(weights_full, axis=-1)
    mixed = mixed * factor[..., None] + jnp.einsum(
        "tkgr,rkd->tkgd",
        weights_full.astype(jnp.bfloat16),
        value_rows,
        preferred_element_type=jnp.float32,
    )
    return (peak_new, total, mixed)


def on_device(
    fresh_queries,
    fresh_keys,
    fresh_values,
    cache,
    pool_root,
    branch_owner,
    branch_len,
    branch_root,
    request_branch,
    token_request,
    residual,
    wo_t,
    norm_gain,
    w_qkv,
):
    seq_count = lax.axis_size("seq")
    root_count = seq_count // 4
    tok_rows = fresh_queries.shape[0]
    kv_local = fresh_keys.shape[1] // HEAD_SIZE
    query_groups = QUERY_HEADS // KEY_VALUE_HEADS
    score_scale = HEAD_SIZE ** (-0.5)
    slot_count = cache.shape[1] - pool_root.shape[1]
    tags = cache_tags(pool_root, branch_owner, branch_len, root_count, slot_count)
    requests = token_request[0]
    local_branches = request_branch[0]
    request_ids = jnp.arange(local_branches.shape[0], dtype=jnp.int32)
    token_branch = jnp.sum(
        jnp.where(requests[:, None] == request_ids[None, :], local_branches[None, :], 0), axis=1
    )
    branch_ids = jnp.arange(branch_root.shape[0], dtype=jnp.int32)
    token_root = jnp.sum(
        jnp.where(token_branch[:, None] == branch_ids[None, :], branch_root[None, :], 0), axis=1
    )
    query_rows = fresh_queries.reshape(tok_rows, kv_local, query_groups, HEAD_SIZE)
    incoming_keys = fresh_keys.reshape(tok_rows, kv_local, HEAD_SIZE)
    incoming_values = fresh_values.reshape(tok_rows, kv_local, HEAD_SIZE)
    positions = jnp.arange(tok_rows, dtype=jnp.int32)
    own_visible = (requests[None, :] == requests[:, None]) & (
        positions[None, :] <= positions[:, None]
    )
    start_state = (
        jnp.full((tok_rows, kv_local, query_groups), -jnp.inf, jnp.float32),
        jnp.zeros((tok_rows, kv_local, query_groups), jnp.float32),
        jnp.zeros((tok_rows, kv_local, query_groups, HEAD_SIZE), jnp.float32),
    )
    start_state = absorb(
        start_state, query_rows, incoming_keys, incoming_values, own_visible, score_scale
    )
    state = start_state
    piece = lax.all_gather(cache, "seq", axis=1, tiled=True)
    rows = piece.shape[1]
    block = 512
    key_blocks = piece[0].reshape(rows // block, block, kv_local, HEAD_SIZE)
    value_blocks = piece[1].reshape(rows // block, block, kv_local, HEAD_SIZE)
    tag_blocks = tags.reshape(rows // block, block)

    def one_block(running, parts):
        key_row_block, value_rows, tag_rows = parts
        visible = (tag_rows[None, :] == token_root[:, None]) | (
            tag_rows[None, :] == root_count + token_branch[:, None]
        )
        updated = absorb(running, query_rows, key_row_block, value_rows, visible, score_scale)
        return (updated, None)

    state, unused = lax.scan(one_block, state, (key_blocks, value_blocks, tag_blocks))
    peak_final, total_final, mixed_final = state
    attn = (
        (mixed_final / total_final[..., None])
        .reshape(tok_rows, kv_local * query_groups * HEAD_SIZE)
        .astype(jnp.bfloat16)
    )
    partial_value = lax.dot_general(
        attn,
        lax.all_gather(wo_t, "seq", axis=0, tiled=True),
        (((1,), (1,)), ((), ())),
        preferred_element_type=jnp.float32,
    )
    summed = lax.psum(partial_value.astype(jnp.bfloat16), "mp").astype(jnp.float32)
    stream = (residual.astype(jnp.float32) + summed).astype(jnp.bfloat16)
    widened = stream.astype(jnp.float32)
    mean_square = jnp.mean(widened * widened, axis=-1, keepdims=True)
    normed = (widened * lax.rsqrt(mean_square + 1e-06) * norm_gain[None, :]).astype(jnp.bfloat16)
    qkv_sum = jnp.dot(
        normed, lax.all_gather(w_qkv, "seq", axis=0, tiled=True), preferred_element_type=jnp.float32
    )
    return (attn, stream, qkv_sum.astype(jnp.bfloat16))


def solution(mesh):
    return jax.shard_map(
        on_device,
        mesh=mesh,
        in_specs=(
            P("seq", "mp"),
            P("seq", "mp"),
            P("seq", "mp"),
            P(None, "seq", "mp"),
            P(),
            P(),
            P(),
            P(),
            P("seq", None),
            P("seq", None),
            P("seq", None),
            P("seq", "mp"),
            P(),
            P("seq", "mp"),
        ),
        out_specs=(P("seq", "mp"), P("seq", None), P("seq", "mp")),
        check_vma=False,
    )
```

profile of v0, /device:TPU:1, one launch (start us, length us, event | category | flops | bytes accessed | tf_op | source)
XLA Modules:
  0.0 339.6 jit_solution(17679690994480268077)
XLA Ops:
  16.6 88.7 %all-gather.4.cloned.1.call-done = bf16[2,8192,256]{2,1,0:T(8,128)(2,1)} async-done(((bf16[2,64,256]{2,1,0:T(8,128)(2,1)}), bf16[2,8192,256]{2,1,0:T(8,128)(2,1)}) %all-gather.4.cloned.1.call-update) | async-done | bytes 8388624 | tf_op jit(solution)/shard_map/all_gather | solution.py:99
  105.3 5.7 %fusion.30 = (bf16[1,8192,256]{2,1,0:T(8,128)(2,1)}, bf16[1,8192,256]{2,1,0:T(8,128)(2,1)}) fusion(bf16[2,8192,256]{2,1,0:T(8,128)(2,1)} %all-gather.4.cloned.1.call-done), kind=kLoop, calls=%fused_computation.64 | loop fusion | bytes 16777216 | tf_op jit(solution)/shard_map/slice | solution.py:103
  111.0 6.9 %reshape.143 = bf16[16,512,2,128]{3,2,1,0:T(2,128)(2,1)} reshape(bf16[1,8192,256]{2,1,0:T(8,128)(2,1)} %get-tuple-element.107) | data formatting | bytes 8388608 | tf_op jit(solution)/shard_map/reshape;squeeze | solution.py:102
  118.0 6.9 %reshape.144 = bf16[16,512,2,128]{3,2,1,0:T(2,128)(2,1)} reshape(bf16[1,8192,256]{2,1,0:T(8,128)(2,1)} %get-tuple-element.106) | data formatting | bytes 8388608 | tf_op jit(solution)/shard_map/reshape;squeeze | solution.py:103
  124.9 39.2 %while.14 = (s32[]{:T(128)}, f32[64,2,2]{0,2,1:T(2,128)S(1)}, f32[64,2,2]{0,2,1:T(2,128)S(1)}, f32[64,2,2,128]{3,0,2,1:T(8,128)S(1)}, s32[16,512]{1,0:T(8,128)S(...) while((s32[]{:T(128)}, f32[64,2,2]{0,2,1:T(2,128)S(1)}, ...), condition=%wide.region_9.10_spmd, body=%wide.region_6.9_spmd.sunk | while | flops 68452928 | bytes 3628149 | solution.py:114
  125.0 1.4 constant_dynamic-slice_fusion.6
  127.5 1.4 constant_dynamic-slice_fusion.6
  129.9 1.4 constant_dynamic-slice_fusion.6
  132.4 1.4 constant_dynamic-slice_fusion.6
  134.8 1.4 constant_dynamic-slice_fusion.6
  137.3 1.4 constant_dynamic-slice_fusion.6
  139.7 1.4 constant_dynamic-slice_fusion.6
  142.2 1.4 constant_dynamic-slice_fusion.6
  144.6 1.4 constant_dynamic-slice_fusion.6
  147.1 1.4 constant_dynamic-slice_fusion.6
  149.5 1.4 constant_dynamic-slice_fusion.6
  152.0 1.4 constant_dynamic-slice_fusion.6
  154.4 1.4 constant_dynamic-slice_fusion.6
  159.3 1.4 constant_dynamic-slice_fusion.6
  164.3 23.8 %all-gather.6.cloned.1.call-done = bf16[2048,512]{1,0:T(8,128)(2,1)} async-done(((bf16[16,512]{1,0:T(8,128)(2,1)}), bf16[2048,512]{1,0:T(8,128)(2,1)}) %all-gather.6.cloned.1.call-update) | async-done | bytes 2097168 | tf_op jit(solution)/shard_map/all_gather | solution.py:123
  188.1 3.0 convolution_convert_fusion
  191.8 46.3 %all-reduce.2.cloned.1.call-done = bf16[64,2048]{1,0:T(8,128)(2,1)} async-done(((bf16[64,2048]{1,0:T(8,128)(2,1)}), bf16[64,2048]{1,0:T(8,128)(2,1)}) %all-reduce.2.cloned.1.call-update) | async-done | bytes 262160 | tf_op jit(solution)/shard_map/psum | solution.py:127
  239.3 90.1 %all-gather.8.cloned.1.call-done = bf16[2048,1024]{1,0:T(8,128)(2,1)} async-done(((bf16[16,1024]{1,0:T(8,128)(2,1)}), bf16[2048,1024]{1,0:T(8,128)(2,1)}) %all-gather.8.cloned.1.call-update) | async-done | bytes 4194320 | tf_op jit(solution)/shard_map/all_gather | solution.py:133
  329.3 3.7 %convolution_convert_fusion.1 = bf16[64,1024]{1,0:T(8,128)(2,1)} fusion(bf16[2048,1024]{1,0:T(8,128)(2,1)} %all-gather.8.cloned.1.call-done, bf16[64,2048]{1,0:T(8,128)(2,1)S(1)} %get-tuple-element.101, f32[2048]{0:T(1024)S(1)} %copy-done.3, f32[64]{0:T(128)S(1)} %add_rsqrt_fusion), kind=kOutput, calls=%fused_computation.22 | convolution fusion | flops 269025280 | bytes 4595968 | tf_op jit(solution)/shard_map/dot_general | solution.py:132
  (185 shorter events, 29.8 us)
Async XLA Ops:
  7.2 98.1 %all-gather.4.cloned.1.call-start = ((), (), s32[]{:S(2)}) async-start(), calls=%async_computation | async-start | bytes 8454144 | tf_op jit(solution)/shard_map/all_gather | solution.py:99
  7.9 180.2 %all-gather.6.cloned.1.call-start = ((), (), s32[]{:S(2)}) async-start(), calls=%async_computation.1 | async-start | bytes 2113536 | tf_op jit(solution)/shard_map/all_gather | solution.py:123
  8.6 229.4 %all-reduce.2.cloned.1.call-start = ((), (), s32[]{:S(2)}) async-start(), calls=%async_computation.2 | async-start | bytes 524288 | tf_op jit(solution)/shard_map/psum | solution.py:127
  124.9 113.2 %copy-start.2 = (bf16[64,2048]{1,0:T(8,128)(2,1)S(1)}, bf16[64,2048]{1,0:T(8,128)(2,1)}, u32[]{:S(2)}) copy-start(bf16[64,2048]{1,0:T(8,128)(2,1)} %param.26) | copy-start | bytes 786436
  124.9 204.4 %copy-start.3 = (f32[2048]{0:T(1024)S(1)}, f32[2048]{0:T(1024)}, u32[]{:S(2)}) copy-start(f32[2048]{0:T(1024)} %param.28) | copy-start | bytes 24580
  164.3 168.7 %copy-start.1 = (bf16[64,512]{1,0:T(8,128)(2,1)}, bf16[64,512]{1,0:T(8,128)(2,1)S(1)}, u32[]{:S(2)}) copy-start(bf16[64,512]{1,0:T(8,128)(2,1)S(1)} %convert_element_type.35) | copy-start | bytes 196612
  191.2 138.1 %all-gather.8.cloned.1.call-start = ((), (), s32[]{:S(2)}) async-start(), calls=%async_computation.3 | async-start | bytes 4227072 | tf_op jit(solution)/shard_map/all_gather | solution.py:133
  239.2 93.8 %copy-start = (bf16[64,2048]{1,0:T(8,128)(2,1)}, bf16[64,2048]{1,0:T(8,128)(2,1)S(1)}, u32[]{:S(2)}) copy-start(bf16[64,2048]{1,0:T(8,128)(2,1)S(1)} %get-tuple-element.101) | copy-start | bytes 786436
Sparse Core Ops, SparseCore 0:
  11.2 94.0 all-gather.3
  108.4 79.6 all-gather.5
  191.3 46.7 all-reduce.1
  241.5 87.7 all-gather.7
where the time goes:
time: 341 us; the launch traced here: 340 us
  waiting for transfers between devices  251 us (74%)
  local copies, waits for them, and re-layouts  44.9 us (13%)
  matrix products  17.1 us (5%)
  between operations  13.9 us (4%)
  other arithmetic  11.8 us (3%)
    all_gather x1, waiting for transfers between devices, on_device(): lax.all_gather(w_qkv, 'seq', axis=0, tiled=True)  90.1 us
    all_gather x1, waiting for transfers between devices, on_device(): piece = lax.all_gather(cache, 'seq', axis=1, tiled=True)  88.7 us
    psum x1, waiting for transfers between devices, on_device(): lax.psum(partial_value.astype(jnp.bfloat16), 'mp').astype(jnp.float32)  46.3 us
    all_gather x1, waiting for transfers between devices, on_device(): lax.all_gather(wo_t, 'seq', axis=0, tiled=True)  23.8 us
    dynamic_slice x32, local copies, waits for them, and re-layouts, on_device(): lax.scan(one_block, state, (key_blocks, value_blocks, tag_blocks))  22.5 us
    another operation x1, local copies, waits for them, and re-layouts, on_device(): value_blocks = piece[1].reshape(rows // block, block, kv_local, HEAD_SIZE)  6.94 us
    another operation x1, local copies, waits for them, and re-layouts, on_device(): key_blocks = piece[0].reshape(rows // block, block, kv_local, HEAD_SIZE)  6.93 us
  transfers between devices with their start and end apart: 4, of which 4 were waited for; matrix products, arithmetic and copies ran while one was open for 20% of the time, Pallas kernels for 0%

commit v1 on v0

--- a/solution.py
+++ b/solution.py
@@ -120,7 +120,9 @@
     )
     partial_value = lax.dot_general(
         attn,
-        lax.all_gather(wo_t, "seq", axis=0, tiled=True),
+        jnp.concatenate(
+            lax.all_to_all(jnp.stack([wo_t] * lax.axis_size("seq")), "seq", 0, 0), axis=0
+        ),
         (((1,), (1,)), ((), ())),
         preferred_element_type=jnp.float32,
     )

time: 341 us -> 346 us (1.015)
  starting transfers between devices: 0.16 us -> 18.5 us
  waiting for transfers between devices: 251 us -> 243 us
  other arithmetic: 11.8 us -> 7.67 us
    all_gather x1 -> x0, waiting for transfers between devices: 23.8 us -> none  [on_device(): lax.all_gather(wo_t, 'seq', axis=0, tiled=True)]
    all_to_all x0 -> x1, starting transfers between devices: none -> 18.4 us  [on_device(): lax.all_to_all(jnp.stack([wo_t] * lax.axis_size('seq')), 'seq', 0, 0)]
    all_gather x1, waiting for transfers between devices: 88.7 us -> 106 us  [on_device(): piece = lax.all_gather(cache, 'seq', axis=1, tiled=True)]
  transfers between devices with their start and end apart: 4 -> 4, of which waited for: 4 -> 3; matrix products, arithmetic and copies ran while one was open for 20% -> 18% of each run, Pallas kernels for 0% -> 0%
where the time goes in v1:
time: 346 us; the launch traced here: 345 us
  waiting for transfers between devices  243 us (70%)
  local copies, waits for them, and re-layouts  44.8 us (13%)
  starting transfers between devices  18.5 us (5%)
  matrix products  15.5 us (4%)
  between operations  14 us (4%)
  other arithmetic  7.67 us (2%)
    all_gather x1, waiting for transfers between devices, on_device(): piece = lax.all_gather(cache, 'seq', axis=1, tiled=True)  106 us
    all_gather x1, waiting for transfers between devices, on_device(): lax.all_gather(w_qkv, 'seq', axis=0, tiled=True)  90.2 us
    psum x1, waiting for transfers between devices, on_device(): lax.psum(partial_value.astype(jnp.bfloat16), 'mp').astype(jnp.float32)  46 us
    dynamic_slice x32, local copies, waits for them, and re-layouts, on_device(): lax.scan(one_block, state, (key_blocks, value_blocks, tag_blocks))  22.5 us
    all_to_all x1, starting transfers between devices, on_device(): lax.all_to_all(jnp.stack([wo_t] * lax.axis_size('seq')), 'seq', 0, 0)  18.4 us
    another operation x1, local copies, waits for them, and re-layouts, on_device(): value_blocks = piece[1].reshape(rows // block, block, kv_local, HEAD_SIZE)  6.96 us
  transfers between devices with their start and end apart: 4, of which 3 were waited for; matrix products, arithmetic and copies ran while one was open for 18% of the time, Pallas kernels for 0%

profile of v1, /device:TPU:1, one launch (start us, length us, event | category | flops | bytes accessed | tf_op | source)
XLA Modules:
  0.0 345.1 jit_solution(3544908710710384154)
XLA Ops:
  8.0 2.3 stack.2
  10.3 18.4 %all-to-all-start = ((bf16[128,16,512]{2,1,0:T(8,128)(2,1)}), bf16[128,16,512]{2,1,0:T(8,128)(2,1)S(1)}, u32[]{:S(2)}, u32[]{:S(2)}) async-start(bf16[128,16,512]{2,1,0:T(8,128)(2,1)} %stack.2), calls=%async_computation | async-start | bytes 4194304 | tf_op jit(solution)/shard_map/all_to_all | solution.py:124
  30.3 106.0 %all-gather.3.cloned.1.call-done = bf16[2,8192,256]{2,1,0:T(8,128)(2,1)} async-done(((bf16[2,64,256]{2,1,0:T(8,128)(2,1)}), bf16[2,8192,256]{2,1,0:T(8,128)(2,1)}) %all-gather.3.cloned.1.call-update) | async-done | bytes 8388624 | tf_op jit(solution)/shard_map/all_gather | solution.py:99
  136.3 5.7 %fusion.30 = (bf16[1,8192,256]{2,1,0:T(8,128)(2,1)}, bf16[1,8192,256]{2,1,0:T(8,128)(2,1)}) fusion(bf16[2,8192,256]{2,1,0:T(8,128)(2,1)} %all-gather.3.cloned.1.call-done), kind=kLoop, calls=%fused_computation.64 | loop fusion | bytes 16777216 | tf_op jit(solution)/shard_map/slice | solution.py:103
  142.0 6.9 %reshape.150 = bf16[16,512,2,128]{3,2,1,0:T(2,128)(2,1)} reshape(bf16[1,8192,256]{2,1,0:T(8,128)(2,1)} %get-tuple-element.107) | data formatting | bytes 8388608 | tf_op jit(solution)/shard_map/reshape;squeeze | solution.py:102
  148.9 7.0 %reshape.151 = bf16[16,512,2,128]{3,2,1,0:T(2,128)(2,1)} reshape(bf16[1,8192,256]{2,1,0:T(8,128)(2,1)} %get-tuple-element.106) | data formatting | bytes 8388608 | tf_op jit(solution)/shard_map/reshape;squeeze | solution.py:103
  155.8 39.2 %while.14 = (s32[]{:T(128)}, f32[64,2,2]{0,2,1:T(2,128)S(1)}, f32[64,2,2]{0,2,1:T(2,128)S(1)}, f32[64,2,2,128]{3,0,2,1:T(8,128)S(1)}, s32[16,512]{1,0:T(8,128)S(...) while((s32[]{:T(128)}, f32[64,2,2]{0,2,1:T(2,128)S(1)}, ...), condition=%wide.region_9.10_spmd, body=%wide.region_6.9_spmd.sunk | while | flops 68452928 | bytes 3628149 | solution.py:114
  155.9 1.4 constant_dynamic-slice_fusion.6
  158.4 1.4 constant_dynamic-slice_fusion.6
  160.8 1.4 constant_dynamic-slice_fusion.6
  163.3 1.4 constant_dynamic-slice_fusion.6
  165.7 1.4 constant_dynamic-slice_fusion.6
  168.2 1.4 constant_dynamic-slice_fusion.6
  170.6 1.4 constant_dynamic-slice_fusion.6
  173.1 1.4 constant_dynamic-slice_fusion.6
  175.5 1.4 constant_dynamic-slice_fusion.6
  178.0 1.4 constant_dynamic-slice_fusion.6
  180.4 1.4 constant_dynamic-slice_fusion.6
  182.9 1.4 constant_dynamic-slice_fusion.6
  187.8 1.4 constant_dynamic-slice_fusion.6
  195.3 1.5 convolution_convert_fusion
  197.5 46.0 %all-reduce.2.cloned.1.call-done = bf16[64,2048]{1,0:T(8,128)(2,1)} async-done(((bf16[64,2048]{1,0:T(8,128)(2,1)}), bf16[64,2048]{1,0:T(8,128)(2,1)}) %all-reduce.2.cloned.1.call-update) | async-done | bytes 262160 | tf_op jit(solution)/shard_map/psum | solution.py:129
  244.6 90.2 %all-gather.5.cloned.1.call-done = bf16[2048,1024]{1,0:T(8,128)(2,1)} async-done(((bf16[16,1024]{1,0:T(8,128)(2,1)}), bf16[2048,1024]{1,0:T(8,128)(2,1)}) %all-gather.5.cloned.1.call-update) | async-done | bytes 4194320 | tf_op jit(solution)/shard_map/all_gather | solution.py:135
  334.8 3.7 %convolution_convert_fusion.1 = bf16[64,1024]{1,0:T(8,128)(2,1)} fusion(bf16[2048,1024]{1,0:T(8,128)(2,1)} %all-gather.5.cloned.1.call-done, bf16[64,2048]{1,0:T(8,128)(2,1)S(1)} %get-tuple-element.101, f32[2048]{0:T(1024)S(1)} %copy-done.7, f32[64]{0:T(128)S(1)} %add_rsqrt_fusion), kind=kOutput, calls=%fused_computation.22 | convolution fusion | flops 269025280 | bytes 4595968 | tf_op jit(solution)/shard_map/dot_general | solution.py:134
  (203 shorter events, 24.2 us)
Async XLA Ops:
  7.2 21.6 %copy-start.3 = (bf16[64,512]{1,0:T(8,128)(2,1)S(1)}, bf16[64,512]{1,0:T(8,128)(2,1)}, u32[]{:S(2)}) copy-start(bf16[64,512]{1,0:T(8,128)(2,1)} %param.16) | copy-start | bytes 196612
  7.2 21.6 %copy-start.4 = (bf16[64,256]{1,0:T(8,128)(2,1)S(1)}, bf16[64,256]{1,0:T(8,128)(2,1)}, u32[]{:S(2)}) copy-start(bf16[64,256]{1,0:T(8,128)(2,1)} %param.17) | copy-start | bytes 98308
  7.2 21.7 %copy-start.5 = (bf16[64,256]{1,0:T(8,128)(2,1)S(1)}, bf16[64,256]{1,0:T(8,128)(2,1)}, u32[]{:S(2)}) copy-start(bf16[64,256]{1,0:T(8,128)(2,1)} %param.18) | copy-start | bytes 98308
  7.2 21.7 %copy-start.9 = (s32[128]{0:T(128)S(1)}, s32[128]{0:T(128)}, u32[]{:S(2)}) copy-start(s32[128]{0:T(128)} %param.21) | copy-start | bytes 1540
  7.2 21.8 %copy-start.10 = (s32[128]{0:T(128)S(1)}, s32[128]{0:T(128)}, u32[]{:S(2)}) copy-start(s32[128]{0:T(128)} %param.22) | copy-start | bytes 1540
  7.2 22.0 %copy-start.6 = (s32[128,32]{0,1:T(8,128)S(1)}, s32[128,32]{0,1:T(8,128)}, u32[]{:S(2)}) copy-start(s32[128,32]{0,1:T(8,128)} %param.20) | copy-start | bytes 49156
  7.2 22.2 %copy-start.8 = (s32[1,64]{1,0:T(1,128)S(1)}, s32[1,64]{1,0:T(1,128)}, u32[]{:S(2)}) copy-start(s32[1,64]{1,0:T(1,128)} %param.25) | copy-start | bytes 772
  7.2 22.2 %copy-start.11 = (s32[1,4]{1,0:T(1,128)S(1)}, s32[1,4]{1,0:T(1,128)}, u32[]{:S(2)}) copy-start(s32[1,4]{1,0:T(1,128)} %param.24) | copy-start | bytes 52
  7.3 22.3 %copy-start.12 = (s32[128]{0:T(128)S(1)}, s32[128]{0:T(128)}, u32[]{:S(2)}) copy-start(s32[128]{0:T(128)} %param.23) | copy-start | bytes 1540
  7.3 129.0 %all-gather.3.cloned.1.call-start = ((), (), s32[]{:S(2)}) async-start(), calls=%async_computation.1 | async-start | bytes 8454144 | tf_op jit(solution)/shard_map/all_gather | solution.py:99
  10.3 184.9 %all-to-all-start = ((bf16[128,16,512]{2,1,0:T(8,128)(2,1)}), bf16[128,16,512]{2,1,0:T(8,128)(2,1)S(1)}, u32[]{:S(2)}, u32[]{:S(2)}) async-start(bf16[128,16,512]{2,1,0:T(8,128)(2,1)} %stack.2), calls=%async_computation | async-start | bytes 4194304 | tf_op jit(solution)/shard_map/all_to_all | solution.py:124
  28.7 214.7 %all-reduce.2.cloned.1.call-start = ((), (), s32[]{:S(2)}) async-start(), calls=%async_computation.2 | async-start | bytes 524288 | tf_op jit(solution)/shard_map/psum | solution.py:129
  155.8 87.7 %copy-start.2 = (bf16[64,2048]{1,0:T(8,128)(2,1)S(1)}, bf16[64,2048]{1,0:T(8,128)(2,1)}, u32[]{:S(2)}) copy-start(bf16[64,2048]{1,0:T(8,128)(2,1)} %param.26) | copy-start | bytes 786436
  155.8 179.0 %copy-start.7 = (f32[2048]{0:T(1024)S(1)}, f32[2048]{0:T(1024)}, u32[]{:S(2)}) copy-start(f32[2048]{0:T(1024)} %param.28) | copy-start | bytes 24580
  195.2 143.3 %copy-start.1 = (bf16[64,512]{1,0:T(8,128)(2,1)}, bf16[64,512]{1,0:T(8,128)(2,1)S(1)}, u32[]{:S(2)}) copy-start(bf16[64,512]{1,0:T(8,128)(2,1)S(1)} %convert_element_type.36) | copy-start | bytes 196612
  196.8 138.1 %all-gather.5.cloned.1.call-start = ((), (), s32[]{:S(2)}) async-start(), calls=%async_computation.3 | async-start | bytes 4227072 | tf_op jit(solution)/shard_map/all_gather | solution.py:135
  244.6 94.0 %copy-start = (bf16[64,2048]{1,0:T(8,128)(2,1)}, bf16[64,2048]{1,0:T(8,128)(2,1)S(1)}, u32[]{:S(2)}) copy-start(bf16[64,2048]{1,0:T(8,128)(2,1)S(1)} %get-tuple-element.101) | copy-start | bytes 786436
Sparse Core Ops, SparseCore 0:
  11.3 124.8 all-gather.2
  196.9 46.5 all-reduce.1
  247.1 87.7 all-gather.4
